TPU v7x, 32 devices: a whole 2x2x4 slice. The times are simulated.
32 devices in a mesh: dap: 8 (over z, x), head: 4 (over y, core).
Axes of the slice: x: 2, y: 2, z: 4, core: 2. Of those that a mesh axis runs over, the one named last changes fastest.
Arguments:
- multiple_aligned_family: bfloat16 [128, 128, 256], P('dap')
- homolog_present_flags: int32 [128], replicated, may hold values from 0 to 1, as said below
- amino_present_flags: int32 [128], replicated, may hold values 0 or 1
- focus_layernorm_scaling: float32 [256], replicated, may hold values from 0.5 to 1.5
- focus_layernorm_offset: float32 [256], replicated, may hold values from -1.8 to 1.8
- combined_focus_matrices: bfloat16 [256, 4, 256], P(None, None, 'head')
- sigmoid_switch_offset: float32 [256], P('head'), may hold values from -4 to 4
- focus_final_matrix: bfloat16 [256, 256], P('head'), may hold values from -0.375 to 0.375
- focus_final_offset: float32 [256], replicated, may hold values from -3 to 3
- tensor_layernorm_scaling: float32 [256], replicated, may hold values from 0.5 to 1.5
- tensor_layernorm_offset: float32 [256], replicated, may hold values from -1.8 to 1.8
- tensor_product_factors: bfloat16 [256, 2, 32], replicated, may hold values from -0.375 to 0.375
- tensor_final_matrix: float32 [1024, 128], replicated, may hold values from -0.1875 to 0.1875
- tensor_final_offset: float32 [128], replicated, may hold values from -4 to 4
Outputs:
- alignment_output: bfloat16 [128, 128, 256], P(('dap', 'head'))
- pair_mean_update: float32 [128, 128, 128], P('dap', 'head')
Inputs may be any that keep to these rules, and one draw needn't show every extreme that they name: homolog_present_flags[0] is always 1.
All inputs are finite; a program needn't handle non-finite values.
Results may differ from a plain program's by a relative error of at most 0.005.
Values may be sent and summed in bfloat16 or wider, within the bound.
A program may use at most 256 MiB of HBM per device.

v0:
```python
import jax
import jax.numpy as jnp
from jax import lax
from jax.sharding import PartitionSpec as P

DH = 32
CO = 32


def layer_norm(value, gain, bias):
    mean = jnp.mean(value, -1, keepdims=True)
    centred = value - mean
    spread = jnp.mean(centred * centred, -1, keepdims=True)
    return centred * lax.rsqrt(spread + 1e-05) * gain + bias


def attend_column(query, keys, values, gate, keep):
    scores = jnp.einsum("shd,thd->hst", query, keys, preferred_element_type=jnp.float32)
    scores = jnp.where(keep[None, None, :], scores, jnp.float32(-1000000000.0))
    top = jnp.max(scores, -1, keepdims=True)
    weights = jnp.exp(scores - top)
    probs = (weights / jnp.sum(weights, -1, keepdims=True)).astype(jnp.bfloat16)
    mixed = jnp.einsum("hst,thd->shd", probs, values, preferred_element_type=jnp.float32)
    return (mixed * gate).astype(jnp.bfloat16)


def per_device(
    multiple_aligned_family,
    homolog_present_flags,
    amino_present_flags,
    focus_layernorm_scaling,
    focus_layernorm_offset,
    combined_focus_matrices,
    sigmoid_switch_offset,
    focus_final_matrix,
    focus_final_offset,
    tensor_layernorm_scaling,
    tensor_layernorm_offset,
    tensor_product_factors,
    tensor_final_matrix,
    tensor_final_offset,
):
    parallel_devices = lax.axis_size("dap")
    n_head = lax.axis_size("head")
    head_id = lax.axis_index("head")
    dap_id = lax.axis_index("dap")
    homolog_shard_number, amino_total, feature_dimension = multiple_aligned_family.shape
    total_seqs = homolog_present_flags.shape[0]
    residue_device_count = amino_total // parallel_devices
    local_heads = sigmoid_switch_offset.shape[0] // DH
    keep = homolog_present_flags > 0
    weights_in = combined_focus_matrices.reshape(feature_dimension, 4 * local_heads * DH)
    gate_shift = sigmoid_switch_offset.reshape(local_heads, DH)
    bundled_focus_units = multiple_aligned_family.reshape(
        homolog_shard_number, parallel_devices, residue_device_count, feature_dimension
    )
    received = lax.all_to_all(bundled_focus_units, "dap", split_axis=1, concat_axis=0, tiled=True)
    block = received[:, 0]
    count = block.shape[1]
    normed = layer_norm(
        block.astype(jnp.float32), focus_layernorm_scaling, focus_layernorm_offset
    ).astype(jnp.bfloat16)
    projected = jnp.dot(
        normed.reshape(total_seqs * count, feature_dimension),
        weights_in,
        preferred_element_type=jnp.float32,
    )
    projected = projected.reshape(total_seqs, count, 4, local_heads, DH)
    query = jnp.moveaxis((projected[:, :, 0] * DH ** (-0.5)).astype(jnp.bfloat16), 1, 0)
    keys = jnp.moveaxis(projected[:, :, 1].astype(jnp.bfloat16), 1, 0)
    values = jnp.moveaxis(projected[:, :, 2].astype(jnp.bfloat16), 1, 0)
    gate = jnp.moveaxis(jax.nn.sigmoid(projected[:, :, 3] + gate_shift), 1, 0)

    def single(operands):
        return attend_column(operands[0], operands[1], operands[2], operands[3], keep)

    attended = lax.map(single, (query, keys, values, gate))
    attended = jnp.moveaxis(attended, 0, 1).reshape(total_seqs * count, local_heads * DH)
    partial_value = jnp.dot(attended, focus_final_matrix, preferred_element_type=jnp.float32)
    partial_value, columns = (
        partial_value.reshape(total_seqs, 1, count, feature_dimension),
        received,
    )
    group = homolog_shard_number // n_head
    columns = columns.reshape(
        parallel_devices, n_head, group, residue_device_count, feature_dimension
    )
    partial_value = partial_value.reshape(
        parallel_devices, n_head, group, residue_device_count, feature_dimension
    )
    summed = lax.psum(partial_value.astype(jnp.bfloat16), "head").astype(jnp.float32)
    summed_mine = lax.dynamic_index_in_dim(summed, head_id, 1, keepdims=True)
    own = lax.dynamic_index_in_dim(columns, head_id, 1, keepdims=True)
    mine = (own.astype(jnp.float32) + summed_mine + focus_final_offset).astype(jnp.bfloat16)
    alignment_rows = lax.all_to_all(
        mine.reshape(parallel_devices * group, residue_device_count, feature_dimension),
        "dap",
        split_axis=0,
        concat_axis=1,
        tiled=True,
    )
    seq_keep = homolog_present_flags.astype(jnp.float32).reshape(parallel_devices, n_head, group)
    row_keep = lax.dynamic_slice_in_dim(
        amino_present_flags, dap_id * residue_device_count, residue_device_count
    ).astype(jnp.float32)
    stack = mine.reshape(parallel_devices * group, residue_device_count, feature_dimension)
    mask_seq = lax.dynamic_index_in_dim(seq_keep, head_id, 1, keepdims=False).reshape(
        parallel_devices * group
    )
    left_weight = tensor_product_factors[:, 0]
    right_weight = tensor_product_factors[:, 1]
    used = stack.shape[0]
    opm_normed = layer_norm(
        stack.astype(jnp.float32), tensor_layernorm_scaling, tensor_layernorm_offset
    ).astype(jnp.bfloat16)
    flat = opm_normed.reshape(used * residue_device_count, feature_dimension)
    keep_rs = mask_seq[:, None, None] * row_keep[None, :, None]
    left = (
        jnp.dot(flat, left_weight, preferred_element_type=jnp.float32).reshape(
            used, residue_device_count, -1
        )
        * keep_rs
    ).astype(jnp.bfloat16)
    right = (
        jnp.dot(flat, right_weight, preferred_element_type=jnp.float32).reshape(
            used, residue_device_count, CO
        )
        * keep_rs
    ).astype(jnp.bfloat16)
    piece = lax.all_gather(right, "dap", axis=1, tiled=True)
    outer = lax.dot_general(
        left, piece, (((0,), (0,)), ((), ())), preferred_element_type=jnp.float32
    )
    outer = outer.transpose(0, 2, 1, 3).reshape(residue_device_count, piece.shape[1], -1)
    partial_pair = jnp.dot(
        outer,
        tensor_final_matrix,
        precision=lax.Precision.HIGHEST,
        preferred_element_type=jnp.float32,
    )
    pair = lax.psum_scatter(partial_pair, "head", scatter_dimension=1, tiled=True)
    col_width = amino_total // n_head
    col_keep = lax.dynamic_slice_in_dim(amino_present_flags, head_id * col_width, col_width).astype(
        jnp.float32
    )
    count = jnp.sum(homolog_present_flags).astype(jnp.float32)
    norm = jnp.maximum(count * row_keep[:, None] * col_keep[None, :], 1.0)
    pair_mean_update = (pair + tensor_final_offset) / norm[:, :, None]
    return (alignment_rows, pair_mean_update)


def solution(mesh):
    return jax.shard_map(
        per_device,
        mesh=mesh,
        in_specs=(
            P("dap", None, None),
            P(),
            P(),
            P(),
            P(),
            P(None, None, "head"),
            P("head"),
            P("head", None),
            P(),
            P(),
            P(),
            P(),
            P(),
            P(),
        ),
        out_specs=(P(("dap", "head"), None, None), P("dap", "head", None)),
        check_vma=False,
    )
```

profile of v0, /device:TPU:0, one launch (start us, length us, event | category | flops | bytes accessed | tf_op | source)
XLA Modules:
  0.0 189.5 jit_solution(11915135432507252343)
XLA Ops:
  7.2 2.4 %copy.23 = bf16[16,8,16,256]{3,2,0,1:T(8,128)(2,1)} copy(bf16[16,8,16,256]{3,2,1,0:T(8,128)(2,1)} %bitcast.152) | data formatting | bytes 2097152 | tf_op jit(solution)/shard_map/reshape | solution.py:54
  9.6 7.4 %all-to-all-start = ((bf16[16,8,16,256]{3,2,0,1:T(8,128)(2,1)}), bf16[16,8,16,256]{3,2,0,1:T(8,128)(2,1)S(1)}, u32[]{:S(2)}, u32[]{:S(2)}) async-start(bf16[16,8,16,256]{3,2,0,1:T(8,128)(2,1)} %copy.23), calls=%async_computation | async-start | bytes 2097152 | tf_op jit(solution)/shard_map/all_to_all | solution.py:57
  17.1 25.6 %all-to-all-done = bf16[16,8,16,256]{3,2,0,1:T(8,128)(2,1)S(1)} async-done(((bf16[16,8,16,256]{3,2,0,1:T(8,128)(2,1)}), bf16[16,8,16,256]{3,2,0,1:T(8,128)(2,1)S(1)}, u32[]{:S(2)}, u32[]{:S(2)}) %all-to-all-start) | async-done | bytes 1048608 | tf_op jit(solution)/shard_map/all_to_all | solution.py:57
  42.8 0.3 convert_reduce_fusion
  43.1 0.7 fusion.43
  43.8 0.7 fusion.46
  44.6 0.3 copy.24
  44.9 0.5 fusion.79
  45.5 0.2 fusion.59
  45.8 10.6 %while.10 = (s32[]{:T(128)}, bf16[16,128,2,32]{1,3,2,0:T(8,128)(2,1)S(1)}, bf16[16,128,2,32]{1,3,2,0:T(8,128)(2,1)S(1)}, pred[128]{0:T(512)(128)(4,1)S(1)}, bf16...) while((s32[]{:T(128)}, ...), condition=%wide.region_5.6_spmd, body=%wide.region_2.5_spmd.sunk | while | flops 6537728 | bytes 137301 | solution.py:77
  45.8 0.3 fusion.98
  46.0 0.4 fusion.99
  46.4 0.3 fusion.98
  46.7 0.4 fusion.99
  47.1 0.3 fusion.98
  47.4 0.4 fusion.99
  47.8 0.3 fusion.98
  48.0 0.4 fusion.99
  48.4 0.3 fusion.98
  48.7 0.4 fusion.99
  49.1 0.3 fusion.98
  49.4 0.4 fusion.99
  49.7 0.3 fusion.98
  50.0 0.4 fusion.99
  50.4 0.3 fusion.98
  50.7 0.4 fusion.99
  51.1 0.3 fusion.98
  51.3 0.4 fusion.99
  51.7 0.3 fusion.98
  52.0 0.4 fusion.99
  52.4 0.3 fusion.98
  52.7 0.4 fusion.99
  53.1 0.3 fusion.98
  53.3 0.4 fusion.99
  53.7 0.3 fusion.98
  54.0 0.4 fusion.99
  54.4 0.3 fusion.98
  54.7 0.4 fusion.99
  55.0 0.3 fusion.98
  55.3 0.4 fusion.99
  55.7 0.3 fusion.98
  56.0 0.4 fusion.99
  56.4 0.9 copy.25
  57.3 0.5 dot_general.33
  57.9 1.4 convolution_convert_fusion
  59.4 0.6 fusion.78
  60.0 0.1 reshape.285
  61.1 33.8 %all-reduce.2.cloned.1.call-done = bf16[8,4,4,16,256]{4,3,2,1,0:T(8,128)(2,1)} async-done(((bf16[8,4,4,16,256]{4,3,2,1,0:T(8,128)(2,1)}), bf16[8,4,4,16,256]{4,3,2,1,0:T(8,128)(2,1)}) %all-reduce.2.cloned.1.call-update) | async-done | bytes 1048592 | tf_op jit(solution)/shard_map/psum | solution.py:91
  94.8 1.7 convert_reduce_fusion.1
  96.6 1.2 fusion.50
  97.9 1.2 fusion.53
  99.0 0.2 fusion.69
  99.2 0.2 fusion.67
  99.4 0.2 copy.33
  99.6 0.2 copy.34
  99.9 33.2 %all_gather.3 = bf16[32,128,32]{0,1,2:T(8,128)(2,1)S(1)} all-gather(bf16[32,16,32]{0,1,2:T(8,128)(2,1)S(1)} %get-tuple-element.61), channel_id=1, replica_groups=mesh['dap'=8,'head'=4] {'dap'}, dimensions={1}, use_global_device_ids=true | all-gather | bytes 294912 | tf_op jit(solution)/shard_map/all_gather | solution.py:130
  133.1 1.3 convolution_bitcast_fusion.1
  134.3 6.5 %copy.28 = f32[16,128,32,32]{1,3,2,0:T(8,128)S(1)} copy(f32[16,128,32,32]{1,2,3,0:T(8,128)S(1)} %convolution_bitcast_fusion.1) | data formatting | bytes 16777216 | tf_op jit(solution)/shard_map/transpose | solution.py:134
  140.8 14.9 %fusion.61 = f32[16,128,128]{2,1,0:T(8,128)} fusion(f32[16,128,1024]{1,2,0:T(8,128)S(1)} %bitcast.147, f32[1024,128]{1,0:T(8,128)S(1)} %copy-done), kind=kOutput, calls=%fused_computation.52 | convolution fusion | flops 3221225472 | bytes 9961472 | tf_op jit(solution)/shard_map/dot_general | solution.py:135
  155.7 5.4 %all-to-all-start.1 = ((bf16[32,16,256]{2,1,0:T(8,128)(2,1)}), bf16[32,16,256]{2,1,0:T(8,128)(2,1)S(1)}, u32[]{:S(2)}, u32[]{:S(2)}) async-start(bf16[32,16,256]{2,1,0:T(8,128)(2,1)} %bitcast.29), calls=%async_computation.1 | async-start | bytes 524288 | tf_op jit(solution)/shard_map/all_to_all | solution.py:95
  161.2 8.1 %all-to-all-done.1 = bf16[32,16,256]{2,1,0:T(8,128)(2,1)S(1)} async-done(((bf16[32,16,256]{2,1,0:T(8,128)(2,1)}), bf16[32,16,256]{2,1,0:T(8,128)(2,1)S(1)}, u32[]{:S(2)}, u32[]{:S(2)}) %all-to-all-start.1) | async-done | bytes 262176 | tf_op jit(solution)/shard_map/all_to_all | solution.py:95
  169.3 0.7 copy.26
  170.0 10.8 %reduce-scatter.2.cloned.1.call-done = f32[16,32,128]{2,1,0:T(8,128)} async-done(((f32[16,128,128]{2,1,0:T(8,128)}), f32[16,32,128]{2,1,0:T(8,128)}) %reduce-scatter.2.cloned.1.call-update) | async-done | bytes 262160 | tf_op jit(solution)/shard_map/reduce_scatter | solution.py:141
  180.8 1.8 add_divide_fusion
  (46 shorter events, 0.9 us)
Async XLA Ops:
  7.2 133.6 %copy-start = (f32[1024,128]{1,0:T(8,128)S(1)}, f32[1024,128]{1,0:T(8,128)}, u32[]{:S(2)}) copy-start(f32[1024,128]{1,0:T(8,128)} %param.28) | copy-start | bytes 1572868
  7.2 9.9 %copy-start.11 = (f32[64]{0:T(128)S(1)}, f32[64]{0:T(128)}, u32[]{:S(2)}) copy-start(f32[64]{0:T(128)} %param.22) | copy-start | bytes 772
  7.2 9.9 %copy-start.12 = (s32[128]{0:T(128)S(1)}, s32[128]{0:T(128)}, u32[]{:S(2)}) copy-start(s32[128]{0:T(128)} %param.17) | copy-start | bytes 1540
  9.6 34.2 %copy-start.4 = (f32[256]{0:T(256)S(1)}, f32[256]{0:T(256)}, u32[]{:S(2)}) copy-start(f32[256]{0:T(256)} %param.20) | copy-start | bytes 3076
  9.6 34.2 %copy-start.5 = (f32[256]{0:T(256)S(1)}, f32[256]{0:T(256)}, u32[]{:S(2)}) copy-start(f32[256]{0:T(256)} %param.19) | copy-start | bytes 3076
  9.6 33.2 %all-to-all-start = ((bf16[16,8,16,256]{3,2,0,1:T(8,128)(2,1)}), bf16[16,8,16,256]{3,2,0,1:T(8,128)(2,1)S(1)}, u32[]{:S(2)}, u32[]{:S(2)}) async-start(bf16[16,8,16,256]{3,2,0,1:T(8,128)(2,1)} %copy.23), calls=%async_computation | async-start | bytes 2097152 | tf_op jit(solution)/shard_map/all_to_all | solution.py:57
  17.0 77.9 %all-reduce.2.cloned.1.call-start = ((), (), s32[]{:S(2)}) async-start(), calls=%async_computation.3 | async-start | bytes 2097152 | tf_op jit(solution)/shard_map/psum | solution.py:91
  43.8 1.1 copy-start.1
  56.4 1.5 copy-start.2
  57.3 3.6 %copy-start.10 = (s32[128]{0:T(128)S(1)}, s32[128]{0:T(128)}, u32[]{:S(2)}) copy-start(s32[128]{0:T(128)} %param.18) | copy-start | bytes 1540
  57.3 37.5 %copy-start.6 = (f32[256]{0:T(256)S(1)}, f32[256]{0:T(256)}, u32[]{:S(2)}) copy-start(f32[256]{0:T(256)} %param.24) | copy-start | bytes 3076
  57.8 40.0 %copy-start.7 = (f32[256]{0:T(256)S(1)}, f32[256]{0:T(256)}, u32[]{:S(2)}) copy-start(f32[256]{0:T(256)} %param.26) | copy-start | bytes 3076
  57.9 40.0 %copy-start.8 = (f32[256]{0:T(256)S(1)}, f32[256]{0:T(256)}, u32[]{:S(2)}) copy-start(f32[256]{0:T(256)} %param.25) | copy-start | bytes 3076
  57.9 41.2 %copy-start.3 = (bf16[256,2,32]{0,2,1:T(8,128)(2,1)S(1)}, bf16[256,2,32]{0,2,1:T(8,128)(2,1)}, u32[]{:S(2)}) copy-start(bf16[256,2,32]{0,2,1:T(8,128)(2,1)} %param.27) | copy-start | bytes 98308
  59.3 121.5 %reduce-scatter.2.cloned.1.call-start = ((), (), s32[]{:S(2)}) async-start(), calls=%async_computation.4 | async-start | bytes 1310720 | tf_op jit(solution)/shard_map/reduce_scatter | solution.py:141
  155.7 25.1 %copy-start.9 = (f32[128]{0:T(128)S(1)}, f32[128]{0:T(128)}, u32[]{:S(2)}) copy-start(f32[128]{0:T(128)} %param.29) | copy-start | bytes 1540
  155.7 13.6 %all-to-all-start.1 = ((bf16[32,16,256]{2,1,0:T(8,128)(2,1)}), bf16[32,16,256]{2,1,0:T(8,128)(2,1)S(1)}, u32[]{:S(2)}, u32[]{:S(2)}) async-start(bf16[32,16,256]{2,1,0:T(8,128)(2,1)} %bitcast.29), calls=%async_computation.1 | async-start | bytes 524288 | tf_op jit(solution)/shard_map/all_to_all | solution.py:95
Sparse Core Ops, SparseCore 0:
  59.5 35.3 all-reduce.1
  155.9 24.9 reduce-scatter.1
where the time goes:
time: 190 us; the launch traced here: 189 us
  waiting for transfers between devices  78.3 us (41%)
  blocking collectives  33.2 us (17%)
  matrix products  29 us (15%)
  between operations  15.1 us (8%)
  starting transfers between devices  12.8 us (7%)
  local copies, waits for them, and re-layouts  12.1 us (6%)
  other arithmetic  8.95 us (5%)
    psum x1, waiting for transfers between devices, per_device(): lax.psum(partial_value.astype(jnp.bfloat16), 'head').astype(jnp.float32)  33.8 us
    all_gather x1, blocking collectives, per_device(): piece = lax.all_gather(right, 'dap', axis=1, tiled=True)  33.2 us
    all_to_all x1, waiting for transfers between devices, per_device(): lax.all_to_all(bundled_focus_units, 'dap', split_axis=1, concat_axis=0, t...  25.6 us
    dot_general x1, matrix products, per_device(): jnp.dot(outer, tensor_final_matrix, precision=lax.Precision.HIGHEST, pref...  14.9 us
    reduce_scatter x1, waiting for transfers between devices, per_device(): lax.psum_scatter(partial_pair, 'head', scatter_dimension=1, tiled=True)  10.8 us
    all_to_all x1, waiting for transfers between devices, per_device(): lax.all_to_all(mine.reshape(parallel_devices * group, residue_device_coun...  8.07 us
    all_to_all x1, starting transfers between devices, per_device(): lax.all_to_all(bundled_focus_units, 'dap', split_axis=1, concat_axis=0, t...  7.41 us
    transpose x1, local copies, waits for them, and re-layouts, per_device(): outer.transpose(0, 2, 1, 3)  6.49 us
  transfers between devices with their start and end apart: 4, of which 4 were waited for; matrix products, arithmetic and copies ran while one was open for 1% of the time, Pallas kernels for 0%

commit v1 on v0

v1 whole, which is shorter than its diff:
```python
import functools

import jax
import jax.numpy as jnp
from jax import lax
from jax.experimental import pallas as pl
from jax.experimental.pallas import tpu as pltpu
from jax.sharding import PartitionSpec as P

DH = 32
CO = 32
F32 = jnp.float32
BF16 = jnp.bfloat16
MESH = pl.DeviceIdType.MESH


def dot(a, b, ca, cb, precision=None):
    return lax.dot_general(
        a, b, (((ca,), (cb,)), ((), ())), preferred_element_type=F32, precision=precision
    )


def iota(shape, dim):
    return lax.broadcasted_iota(jnp.int32, shape, dim)


def one_hot(hit):
    return jnp.where(hit, 1.0, 0.0).astype(BF16)


def layer_norm(value, gain, bias):
    mean = jnp.mean(value, -1, keepdims=True)
    centred = value - mean
    spread = jnp.mean(centred * centred, -1, keepdims=True)
    return centred * lax.rsqrt(spread + 1e-05) * gain + bias


def kernel(
    nd,
    nh,
    msa,
    homolog,
    amino,
    gain1,
    bias1,
    w_local,
    gate_local,
    wf_local,
    final_bias,
    gain2,
    bias2,
    factors,
    w_pair,
    pair_bias,
    align_out,
    pair_out,
    send1,
    recv1,
    w_all,
    wf_all,
    gate_col,
    gate_all,
    aligned,
    cbuf,
    crecv,
    lbuf,
    rstack,
    rbuf,
    left_all,
    right_all,
    w_r,
    obuf,
    s1,
    r1,
    s2,
    r2,
    s3,
    r3,
    s4,
    r4,
    s5,
    r5,
):
    md = lax.axis_index("dap")
    mh = lax.axis_index("head")
    sl, res, ch = msa.shape
    seqs = sl * nd
    rb = res // nd
    rd = rb // nh
    sg = sl // nh
    n = nd * nh
    hl = gate_local.shape[1]
    heads = hl * nh // DH
    dg = nd // nh
    ein = 16 // rd
    neb = CO // ein
    cz = w_pair.shape[1]
    me = md * nh + mh
    rows = rd * sl

    def peer(k):
        t = lax.rem(me + k, n)
        return t // nh, lax.rem(t, nh)

    barrier = pltpu.get_barrier_semaphore()
    for k in range(1, n):
        pl.semaphore_signal(barrier, inc=1, device_id=peer(k), device_id_type=MESH)

    ri = iota((rows, sl * rb), 0)
    ci = iota((rows, sl * rb), 1)
    pick = one_hot(ci == lax.rem(ri, sl) * rb + mh * rd + ri // sl)
    for d in range(nd):
        block = msa[:, d * rb : (d + 1) * rb, :].reshape(sl * rb, ch)
        send1[d] = dot(pick, block, 1, 0).astype(BF16)
    eye = jnp.where(iota((hl, hl), 0) == iota((hl, hl), 1), 1.0, 0.0).astype(F32)
    gate_col[...] = dot(
        eye, jnp.broadcast_to(gate_local[...], (128, hl)), 1, 1, lax.Precision.HIGHEST
    )
    pl.semaphore_wait(barrier, n - 1)

    copies = []

    def start(src, dst, ss, rs, to):
        c = pltpu.make_async_remote_copy(
            src_ref=src, dst_ref=dst, send_sem=ss, recv_sem=rs, device_id=to, device_id_type=MESH
        )
        c.start()
        copies.append(c)
        return c

    mine = pl.ds(pl.multiple_of(mh * hl, hl), hl)
    weights = []
    msas = []
    for k in range(1, nh):
        to = (md, lax.rem(mh + k, nh))
        weights.append(start(w_local, w_all.at[:, mine, :], s2.at[k, 0], r2.at[k, 0], to))
        weights.append(start(wf_local, wf_all.at[mine, :], s2.at[k, 1], r2.at[k, 1], to))
        weights.append(start(gate_col, gate_all.at[mine, :], s2.at[k, 2], r2.at[k, 2], to))
    for k in range(1, nd):
        to = lax.rem(md + k, nd)
        msas.append(start(send1.at[to], recv1.at[md], s1.at[k], r1.at[k], (to, mh)))

    recv1[md] = send1[md]
    w_all[:, mine, :] = w_local[...]
    wf_all[mine, :] = wf_local[...]
    gate_all[mine, :] = gate_col[...]
    for eb in range(neb):
        for e in range(ein):
            w_r[eb * CO : (eb + 1) * CO, e * cz : (e + 1) * cz] = w_pair[
                pl.ds(eb * ein + e, CO, stride=CO), :
            ].astype(BF16)
    seq_row = homolog[...].astype(F32)
    res_row = amino[...].astype(F32)
    count = jnp.sum(seq_row, axis=1, keepdims=True)
    seq_wide = jnp.broadcast_to(seq_row, (128, seqs)).astype(BF16)
    res_wide = jnp.broadcast_to(res_row, (128, res)).astype(BF16)
    seq_eye = one_hot(iota((seqs, seqs), 0) == iota((seqs, seqs), 1))
    seq_col = dot(seq_eye, seq_wide, 1, 1)[:, :1]
    penalty = jnp.broadcast_to(jnp.where(seq_col > 0.5, 0.0, -1e9), (seqs, seqs))
    own = one_hot(iota((8, res), 1) == md * rb + mh * rd + iota((8, res), 0))
    own_keep = dot(own, res_wide, 1, 1)[:, :1]
    for c in weights:
        c.wait_recv()
    for c in msas:
        c.wait_recv()

    for r in range(rd):
        x = recv1[:, r * sl : (r + 1) * sl, :].reshape(seqs, ch).astype(F32)
        normed = layer_norm(x, gain1[...], bias1[...]).astype(BF16)
        q = (dot(w_all[0], normed, 1, 1) * DH ** (-0.5)).astype(BF16)
        key = dot(w_all[1], normed, 1, 1).astype(BF16)
        val = dot(w_all[2], normed, 1, 1).astype(BF16)
        gate = jax.nn.sigmoid(dot(w_all[3], normed, 1, 1) + gate_all[:, :1])
        parts = []
        for h in range(heads):
            at = slice(h * DH, (h + 1) * DH)
            scores = dot(key[at], q[at], 0, 0) + penalty
            top = jnp.max(scores, 0, keepdims=True)
            w = jnp.exp(scores - top)
            total = jnp.sum(w, 0, keepdims=True)
            probs = (w * (1.0 / total)).astype(BF16)
            parts.append((dot(val[at], probs, 1, 0) * gate[at]).astype(BF16))
        attended = jnp.concatenate(parts, 0)
        update = dot(attended, wf_all[...], 0, 0)
        out = (x + update + final_bias[...]).astype(BF16)
        aligned[r] = out
        opm = layer_norm(out.astype(F32), gain2[...], bias2[...]).astype(BF16)
        both = dot(factors[...], opm, 1, 1) * (seq_row * own_keep[r : r + 1])
        lbuf[r * CO : (r + 1) * CO, :] = both[:CO].astype(BF16)
        rstack[r * CO : (r + 1) * CO, :] = both[CO:].astype(BF16)

    nr = rd * CO
    ri = iota((nr, nr), 0)
    mix = one_hot(iota((nr, nr), 1) == lax.rem(ri, rd) * CO + ri // rd)
    rbuf[...] = dot(mix, rstack[...], 1, 0).astype(BF16).reshape(rbuf.shape)
    to_h = md // dg
    slot = lax.rem(md, dg) * nh + mh
    spot = pl.ds(pl.multiple_of(slot * 16, 16), 16)

    def right_copy(k):
        return pltpu.make_async_remote_copy(
            src_ref=rbuf,
            dst_ref=right_all.at[:, spot, :],
            send_sem=s4.at[k],
            recv_sem=r4.at[slot],
            device_id=(lax.rem(md + k, nd), to_h),
            device_id_type=MESH,
        )

    @pl.when(to_h == mh)
    def _():
        right_all[:, spot, :] = rbuf[...]

    @pl.when(to_h != mh)
    def _():
        right_copy(0).start()

    for k in range(1, nd):
        right_copy(k).start()
    lefts = []
    for k in range(1, nh):
        to = (md, lax.rem(mh + k, nh))
        lefts.append(start(lbuf, left_all.at[mh], s5.at[k], r5.at[k], to))
    left_all[mh] = lbuf[...]

    ri = iota((rows, rows), 0)
    chunk = sg * rd
    col = lax.rem(ri, rd) * sl + (ri // chunk) * sg + lax.rem(ri, chunk) // rd
    order = one_hot(iota((rows, rows), 1) == col)
    for d in range(nd):
        block = aligned[:, d * sl : (d + 1) * sl, :].reshape(rows, ch)
        cbuf[d * nh : (d + 1) * nh] = dot(order, block, 1, 0).astype(BF16).reshape(nh, chunk, ch)
    outs = []
    for k in range(1, n):
        to = peer(k)
        outs.append(start(cbuf.at[lax.rem(me + k, n)], crecv.at[me], s3.at[k], r3.at[k], to))
    crecv[me] = cbuf[me]

    for c in lefts:
        c.wait_recv()
    for i in range(dg * nh):
        from_d = mh * dg + i // nh

        @pl.when(jnp.logical_or(from_d != md, i % nh != mh))
        def _():
            pltpu.make_async_remote_copy(
                src_ref=rbuf,
                dst_ref=right_all.at[:, i * 16 : (i + 1) * 16, :],
                send_sem=s4.at[0],
                recv_sem=r4.at[i],
                device_id=(md, to_h),
                device_id_type=MESH,
            ).wait_recv()

    left = left_all[...].reshape(nh * nr, seqs)
    for eb in range(neb):
        obuf[:, eb] = dot(left, right_all[eb], 1, 1).astype(BF16).reshape(rb, CO, -1)
    lanes = right_all.shape[1]
    cols = lanes // ein
    pick_i = one_hot(iota((rb, res), 1) == md * rb + iota((rb, res), 0))
    pick_j = one_hot(iota((cols, res), 1) == mh * cols + iota((cols, res), 0))
    keep_i = dot(pick_i, res_wide, 1, 1)[:, :cz]
    keep_j = dot(pick_j, res_wide, 1, 1)[:, :cz]
    group = lax.rem(iota((lanes, cz), 0), 16) // rd
    low = iota((8, cz), 0) < rd
    for i in range(rb):
        o = obuf[i].reshape(neb * CO, lanes)
        wide = dot(o, w_r[...], 0, 0)
        t = jnp.where(group == 0, wide[:, :cz], 0.0)
        for e in range(1, ein):
            t = jnp.where(group == e, wide[:, e * cz : (e + 1) * cz], t)
        t = t.reshape(lanes // 16, 2, 8, cz)
        u = t[:, 0] + t[:, 1]
        scale = 1.0 / jnp.maximum(count * keep_i[i : i + 1] * keep_j, 1.0)
        for g in range(cols // 8):
            a = u[2 * g]
            b = u[2 * g + 1]
            v = jnp.where(low, a + pltpu.roll(a, 4, 0), b + pltpu.roll(b, 4, 0))
            at = slice(g * 8, (g + 1) * 8)
            pair_out[i, at, :] = (v + pair_bias[...]) * scale[at]

    for c in outs:
        c.wait_recv()
    ri = iota((rows, rows), 0)
    wide_chunk = nh * rd
    col = lax.rem(ri, wide_chunk) // rd * chunk + ri // wide_chunk * rd + lax.rem(ri, rd)
    order = one_hot(iota((rows, rows), 1) == col)
    for d in range(nd):
        block = crecv[d * nh : (d + 1) * nh].reshape(rows, ch)
        align_out[:, d * rb : (d + 1) * rb, :] = (
            dot(order, block, 1, 0).astype(BF16).reshape(sg, rb, ch)
        )

    for c in copies:
        c.wait_send()

    @pl.when(to_h != mh)
    def _():
        right_copy(0).wait_send()

    for k in range(1, nd):
        right_copy(k).wait_send()


def per_device(
    nd,
    nh,
    multiple_aligned_family,
    homolog_present_flags,
    amino_present_flags,
    focus_layernorm_scaling,
    focus_layernorm_offset,
    combined_focus_matrices,
    sigmoid_switch_offset,
    focus_final_matrix,
    focus_final_offset,
    tensor_layernorm_scaling,
    tensor_layernorm_offset,
    tensor_product_factors,
    tensor_final_matrix,
    tensor_final_offset,
):
    sl, res, ch = multiple_aligned_family.shape
    seqs = homolog_present_flags.shape[0]
    hl = sigmoid_switch_offset.shape[0]
    cz = tensor_final_matrix.shape[1]
    rb = res // nd
    rd = rb // nh
    sg = sl // nh
    n = nd * nh
    ein = 16 // rd
    neb = CO // ein
    cols = res // nh
    row = lambda v: v.reshape(1, -1)
    w_local = combined_focus_matrices.transpose(1, 2, 0)
    factors = tensor_product_factors.transpose(1, 2, 0).reshape(2 * CO, ch)
    dma = pltpu.SemaphoreType.DMA
    vmem = pl.BlockSpec(memory_space=pltpu.VMEM)
    return pl.pallas_call(
        functools.partial(kernel, nd, nh),
        out_shape=(
            jax.ShapeDtypeStruct((sg, res, ch), BF16),
            jax.ShapeDtypeStruct((rb, cols, cz), F32),
        ),
        in_specs=[vmem] * 14,
        out_specs=(vmem, vmem),
        scratch_shapes=[
            pltpu.VMEM((nd, rd * sl, ch), BF16),
            pltpu.VMEM((nd, rd * sl, ch), BF16),
            pltpu.VMEM((4, nh * hl, ch), BF16),
            pltpu.VMEM((nh * hl, ch), BF16),
            pltpu.VMEM((hl, 128), F32),
            pltpu.VMEM((nh * hl, 128), F32),
            pltpu.VMEM((rd, seqs, ch), BF16),
            pltpu.VMEM((n, sg * rd, ch), BF16),
            pltpu.VMEM((n, sg * rd, ch), BF16),
            pltpu.VMEM((rd * CO, seqs), BF16),
            pltpu.VMEM((rd * CO, seqs), BF16),
            pltpu.VMEM((neb, 16, seqs), BF16),
            pltpu.VMEM((nh, rd * CO, seqs), BF16),
            pltpu.VMEM((neb, cols * ein, seqs), BF16),
            pltpu.VMEM((neb * CO, ein * cz), BF16),
            pltpu.VMEM((rb, neb, CO, cols * ein), BF16),
            dma((nd,)),
            dma((nd,)),
            dma((nh, 3)),
            dma((nh, 3)),
            dma((n,)),
            dma((n,)),
            dma((nd,)),
            dma((nd,)),
            dma((nh,)),
            dma((nh,)),
        ],
        compiler_params=pltpu.CompilerParams(
            collective_id=0, has_side_effects=True, vmem_limit_bytes=56 * 1024 * 1024
        ),
    )(
        multiple_aligned_family,
        row(homolog_present_flags),
        row(amino_present_flags),
        row(focus_layernorm_scaling),
        row(focus_layernorm_offset),
        w_local,
        row(sigmoid_switch_offset),
        focus_final_matrix,
        row(focus_final_offset),
        row(tensor_layernorm_scaling),
        row(tensor_layernorm_offset),
        factors,
        tensor_final_matrix,
        row(tensor_final_offset),
    )


def solution(mesh):
    nd = mesh.shape["dap"]
    nh = mesh.shape["head"]
    return jax.shard_map(
        functools.partial(per_device, nd, nh),
        mesh=mesh,
        in_specs=(
            P("dap", None, None),
            P(),
            P(),
            P(),
            P(),
            P(None, None, "head"),
            P("head"),
            P("head", None),
            P(),
            P(),
            P(),
            P(),
            P(),
            P(),
        ),
        out_specs=(P(("dap", "head"), None, None), P("dap", "head", None)),
        check_vma=False,
    )
```

time: 190 us -> 43.6 us (0.23)
  waiting for transfers between devices: 78.3 us -> 0 us
  Pallas kernels: 0 us -> 40.4 us
  blocking collectives: 33.2 us -> 0 us
  matrix products: 29 us -> 0 us
  between operations: 15.1 us -> 0.65 us
  starting transfers between devices: 12.8 us -> 0 us
  local copies, waits for them, and re-layouts: 12.1 us -> 2.42 us
  other arithmetic: 8.95 us -> 0 us
    pallas_call x0 -> x1, Pallas kernels: none -> 40.4 us  [per_device(): pl.pallas_call(functools.partial(kernel, nd, nh), out_shape=(jax.ShapeDty...]
    psum x1 -> x0, waiting for transfers between devices: 33.8 us -> none  [per_device(): lax.psum(partial_value.astype(jnp.bfloat16), 'head').astype(jnp.float32)]
    all_to_all x2 -> x0, waiting for transfers between devices: 33.7 us -> none  [the longest x1 25.6 us: per_device(): lax.all_to_all(bundled_focus_units, 'dap', split_axis=1, concat_axis=0, t...]
    all_gather x1 -> x0, blocking collectives: 33.2 us -> none  [per_device(): piece = lax.all_gather(right, 'dap', axis=1, tiled=True)]
    dot_general x22 -> x0, matrix products: 24.6 us -> none  [the longest x1 14.9 us: per_device(): jnp.dot(outer, tensor_final_matrix, precision=lax.Precision.HIGHEST, pref...]
    all_to_all x2 -> x0, starting transfers between devices: 12.8 us -> none  [the longest x1 7.41 us: per_device(): lax.all_to_all(bundled_focus_units, 'dap', split_axis=1, concat_axis=0, t...]
    reduce_scatter x1 -> x0, waiting for transfers between devices: 10.8 us -> none  [per_device(): lax.psum_scatter(partial_pair, 'head', scatter_dimension=1, tiled=True)]
    transpose x3 -> x0, local copies, waits for them, and re-layouts: 7.45 us -> none  [the longest x1 6.49 us: per_device(): outer.transpose(0, 2, 1, 3)]
  transfers between devices with their start and end apart: 4 -> 0, of which waited for: 4 -> 0; matrix products, arithmetic and copies ran while one was open for 1% -> 0% of each run, Pallas kernels for 0% -> 0%
where the time goes in v1:
time: 43.6 us; the launch traced here: 43.5 us
  Pallas kernels  40.4 us (93%)
  local copies, waits for them, and re-layouts  2.42 us (6%)
  between operations  0.65 us (1%)
    pallas_call x1, Pallas kernels, per_device(): pl.pallas_call(functools.partial(kernel, nd, nh), out_shape=(jax.ShapeDty...  40.4 us
    unnamed x4, local copies, waits for them, and re-layouts  2.42 us

profile of v1, /device:TPU:0, one launch (start us, length us, event | category | flops | bytes accessed | tf_op | source)
XLA Modules:
  0.0 43.5 jit_solution(6391921024003617962)
XLA Ops:
  0.6 40.4 %shard_map.149 = (bf16[4,128,256]{2,1,0:T(8,128)(2,1)}, f32[16,32,128]{2,1,0:T(8,128)}) custom-call(bf16[16,128,256]{2,1,0:T(8,128)(2,1)} %msa.1, s32[1,128]{1,0:T(1,128)} %bitcast.20, s32[1,128]{1,0:T(1,128)} %bitcast.21, f32[1,256]{1,0:T(1,128)} %bitcast.15, f32[1,256]{1,0:T(1,128)} %bitcast.16, bf16[4,64,256]{2,1,0:T(8,128)(2,1)} %bitcast.13, ...), custom_call_target="tpu_custom_call" | custom-call | tf_op jit(solution)/shard_map/pallas_call | solution.py:339
  41.0 0.0 copy-start
  41.0 1.7 %copy.18 = bf16[4,128,256]{2,1,0:T(8,128)(2,1)} copy(bf16[4,128,256]{2,1,0:T(8,128)(2,1)} %get-tuple-element.4) | data formatting | bytes 524288
  42.7 0.0 copy-done
  42.7 0.7 %copy.19 = f32[16,32,128]{2,1,0:T(8,128)} copy(f32[16,32,128]{2,1,0:T(8,128)S(1)} %copy-done) | data formatting | bytes 524288
Async XLA Ops:
  41.0 1.7 %copy-start = (f32[16,32,128]{2,1,0:T(8,128)S(1)}, f32[16,32,128]{2,1,0:T(8,128)}, u32[]{:S(2)}) copy-start(f32[16,32,128]{2,1,0:T(8,128)} %get-tuple-element.5) | copy-start | bytes 786436

commit v2 on v1

--- a/solution.py
+++ b/solution.py
@@ -58,14 +58,14 @@
     recv1,
     w_all,
     wf_all,
-    gate_col,
+    gate_rows,
     gate_all,
     aligned,
     cbuf,
     crecv,
     lbuf,
     rstack,
-    rbuf,
+    right_in,
     left_all,
     right_all,
     w_r,
@@ -103,8 +103,13 @@
         return t // nh, lax.rem(t, nh)
 
     barrier = pltpu.get_barrier_semaphore()
-    for k in range(1, n):
-        pl.semaphore_signal(barrier, inc=1, device_id=peer(k), device_id_type=MESH)
+    partner = mh + 1 - 2 * lax.rem(mh, 2)
+    for k in range(1, nh):
+        to = (md, lax.rem(mh + k, nh))
+        pl.semaphore_signal(barrier, inc=1, device_id=to, device_id_type=MESH)
+    for k in range(1, nd):
+        to = (lax.rem(md + k, nd), mh)
+        pl.semaphore_signal(barrier, inc=1, device_id=to, device_id_type=MESH)
 
     ri = iota((rows, sl * rb), 0)
     ci = iota((rows, sl * rb), 1)
@@ -112,11 +117,7 @@
     for d in range(nd):
         block = msa[:, d * rb : (d + 1) * rb, :].reshape(sl * rb, ch)
         send1[d] = dot(pick, block, 1, 0).astype(BF16)
-    eye = jnp.where(iota((hl, hl), 0) == iota((hl, hl), 1), 1.0, 0.0).astype(F32)
-    gate_col[...] = dot(
-        eye, jnp.broadcast_to(gate_local[...], (128, hl)), 1, 1, lax.Precision.HIGHEST
-    )
-    pl.semaphore_wait(barrier, n - 1)
+    pl.semaphore_wait(barrier, nd + nh - 2)
 
     copies = []
 
@@ -128,22 +129,52 @@
         copies.append(c)
         return c
 
-    mine = pl.ds(pl.multiple_of(mh * hl, hl), hl)
-    weights = []
+    def head_rows(g):
+        return pl.ds(pl.multiple_of(g * hl, hl), hl)
+
+    def send_weights(g, own, idx, to):
+        at = head_rows(g)
+        src = (
+            (w_local, wf_local, gate_local)
+            if own
+            else (w_all.at[:, at, :], wf_all.at[at, :], gate_rows.at[g])
+        )
+        dst = (w_all.at[:, at, :], wf_all.at[at, :], gate_rows.at[g])
+        for j in range(3):
+            start(src[j], dst[j], s2.at[idx, j], r2.at[g, j], (md, to))
+
+    def wait_weights(g):
+        at = head_rows(g)
+        src = (w_local, wf_local, gate_local)
+        dst = (w_all.at[:, at, :], wf_all.at[at, :], gate_rows.at[g])
+        for j in range(3):
+            pltpu.make_async_remote_copy(
+                src_ref=src[j],
+                dst_ref=dst[j],
+                send_sem=s2.at[0, j],
+                recv_sem=r2.at[g, j],
+                device_id=(md, partner),
+                device_id_type=MESH,
+            ).wait_recv()
+
+    mine = head_rows(mh)
+    pairs = nh // 2
+    for k in range(1, pairs):
+        send_weights(mh, True, k, lax.rem(mh + 2 * k, nh))
+    send_weights(mh, True, 0, partner)
     msas = []
-    for k in range(1, nh):
-        to = (md, lax.rem(mh + k, nh))
-        weights.append(start(w_local, w_all.at[:, mine, :], s2.at[k, 0], r2.at[k, 0], to))
-        weights.append(start(wf_local, wf_all.at[mine, :], s2.at[k, 1], r2.at[k, 1], to))
-        weights.append(start(gate_col, gate_all.at[mine, :], s2.at[k, 2], r2.at[k, 2], to))
-    for k in range(1, nd):
-        to = lax.rem(md + k, nd)
-        msas.append(start(send1.at[to], recv1.at[md], s1.at[k], r1.at[k], (to, mh)))
+    for r in range(rd):
+        at = slice(r * sl, (r + 1) * sl)
+        for k in range(1, nd):
+            to = lax.rem(md + k, nd)
+            msas.append(
+                start(send1.at[to, at], recv1.at[md, at], s1.at[k, r], r1.at[k, r], (to, mh))
+            )
 
     recv1[md] = send1[md]
     w_all[:, mine, :] = w_local[...]
     wf_all[mine, :] = wf_local[...]
-    gate_all[mine, :] = gate_col[...]
+    gate_rows[mh] = gate_local[...]
     for eb in range(neb):
         for e in range(ein):
             w_r[eb * CO : (eb + 1) * CO, e * cz : (e + 1) * cz] = w_pair[
@@ -159,12 +190,37 @@
     penalty = jnp.broadcast_to(jnp.where(seq_col > 0.5, 0.0, -1e9), (seqs, seqs))
     own = one_hot(iota((8, res), 1) == md * rb + mh * rd + iota((8, res), 0))
     own_keep = dot(own, res_wide, 1, 1)[:, :1]
-    for c in weights:
-        c.wait_recv()
-    for c in msas:
-        c.wait_recv()
+    for k in range(1, pairs):
+        g = lax.rem(mh + nh - 2 * k, nh)
+        wait_weights(g)
+        send_weights(g, False, pairs - 1 + k, partner)
+    wait_weights(partner)
+    for k in range(1, pairs):
+        wait_weights(lax.rem(partner + nh - 2 * k, nh))
+    eye = jnp.where(iota((hl, hl), 0) == iota((hl, hl), 1), 1.0, 0.0).astype(F32)
+    for g in range(nh):
+        wide = jnp.broadcast_to(gate_rows[g], (128, hl))
+        gate_all[g * hl : (g + 1) * hl, :] = dot(eye, wide, 1, 1, lax.Precision.HIGHEST)
+
+    to_h = md // dg
+    slot = lax.rem(md, dg) * nh + mh
+
+    def right_copy(k, r, i):
+        at = slice(r * CO, (r + 1) * CO)
+        return pltpu.make_async_remote_copy(
+            src_ref=rstack.at[at, :],
+            dst_ref=right_in.at[i, at, :],
+            send_sem=s4.at[k, r],
+            recv_sem=r4.at[i, r],
+            device_id=(lax.rem(md + k, nd), to_h),
+            device_id_type=MESH,
+        )
+
+    lefts = []
 
     for r in range(rd):
+        for c in msas[r * (nd - 1) : (r + 1) * (nd - 1)]:
+            c.wait_recv()
         x = recv1[:, r * sl : (r + 1) * sl, :].reshape(seqs, ch).astype(F32)
         normed = layer_norm(x, gain1[...], bias1[...]).astype(BF16)
         q = (dot(w_all[0], normed, 1, 1) * DH ** (-0.5)).astype(BF16)
@@ -189,38 +245,24 @@
         lbuf[r * CO : (r + 1) * CO, :] = both[:CO].astype(BF16)
         rstack[r * CO : (r + 1) * CO, :] = both[CO:].astype(BF16)
 
-    nr = rd * CO
-    ri = iota((nr, nr), 0)
-    mix = one_hot(iota((nr, nr), 1) == lax.rem(ri, rd) * CO + ri // rd)
-    rbuf[...] = dot(mix, rstack[...], 1, 0).astype(BF16).reshape(rbuf.shape)
-    to_h = md // dg
-    slot = lax.rem(md, dg) * nh + mh
-    spot = pl.ds(pl.multiple_of(slot * 16, 16), 16)
-
-    def right_copy(k):
-        return pltpu.make_async_remote_copy(
-            src_ref=rbuf,
-            dst_ref=right_all.at[:, spot, :],
-            send_sem=s4.at[k],
-            recv_sem=r4.at[slot],
-            device_id=(lax.rem(md + k, nd), to_h),
-            device_id_type=MESH,
-        )
+        at = slice(r * CO, (r + 1) * CO)
+
+        @pl.when(to_h != mh)
+        def _():
+            right_copy(0, r, slot).start()
+
+        for k in range(1, nd):
+            right_copy(k, r, slot).start()
+        for k in range(1, nh):
+            to = (md, lax.rem(mh + k, nh))
+            lefts.append(
+                start(lbuf.at[at, :], left_all.at[mh, at, :], s5.at[k, r], r5.at[k, r], to)
+            )
 
     @pl.when(to_h == mh)
     def _():
-        right_all[:, spot, :] = rbuf[...]
-
-    @pl.when(to_h != mh)
-    def _():
-        right_copy(0).start()
-
-    for k in range(1, nd):
-        right_copy(k).start()
-    lefts = []
-    for k in range(1, nh):
-        to = (md, lax.rem(mh + k, nh))
-        lefts.append(start(lbuf, left_all.at[mh], s5.at[k], r5.at[k], to))
+        right_in[slot] = rstack[...]
+
     left_all[mh] = lbuf[...]
 
     ri = iota((rows, rows), 0)
@@ -238,19 +280,19 @@
 
     for c in lefts:
         c.wait_recv()
+    nr = rd * CO
+    ri = iota((nr, nr), 0)
+    mix = one_hot(iota((nr, nr), 1) == lax.rem(ri, rd) * CO + ri // rd)
     for i in range(dg * nh):
         from_d = mh * dg + i // nh
 
         @pl.when(jnp.logical_or(from_d != md, i % nh != mh))
         def _():
-            pltpu.make_async_remote_copy(
-                src_ref=rbuf,
-                dst_ref=right_all.at[:, i * 16 : (i + 1) * 16, :],
-                send_sem=s4.at[0],
-                recv_sem=r4.at[i],
-                device_id=(md, to_h),
-                device_id_type=MESH,
-            ).wait_recv()
+            for r in range(rd):
+                right_copy(0, r, i).wait_recv()
+
+        part = dot(mix, right_in[i], 1, 0).astype(BF16)
+        right_all[:, i * 16 : (i + 1) * 16, :] = part.reshape(neb, 16, seqs)
 
     left = left_all[...].reshape(nh * nr, seqs)
     for eb in range(neb):
@@ -294,12 +336,14 @@
     for c in copies:
         c.wait_send()
 
-    @pl.when(to_h != mh)
-    def _():
-        right_copy(0).wait_send()
-
-    for k in range(1, nd):
-        right_copy(k).wait_send()
+    for r in range(rd):
+
+        @pl.when(to_h != mh)
+        def _():
+            right_copy(0, r, slot).wait_send()
+
+        for k in range(1, nd):
+            right_copy(k, r, slot).wait_send()
 
 
 def per_device(
@@ -349,28 +393,28 @@
             pltpu.VMEM((nd, rd * sl, ch), BF16),
             pltpu.VMEM((4, nh * hl, ch), BF16),
             pltpu.VMEM((nh * hl, ch), BF16),
-            pltpu.VMEM((hl, 128), F32),
+            pltpu.VMEM((nh, 1, hl), F32),
             pltpu.VMEM((nh * hl, 128), F32),
             pltpu.VMEM((rd, seqs, ch), BF16),
             pltpu.VMEM((n, sg * rd, ch), BF16),
             pltpu.VMEM((n, sg * rd, ch), BF16),
             pltpu.VMEM((rd * CO, seqs), BF16),
             pltpu.VMEM((rd * CO, seqs), BF16),
-            pltpu.VMEM((neb, 16, seqs), BF16),
+            pltpu.VMEM((nd, rd * CO, seqs), BF16),
             pltpu.VMEM((nh, rd * CO, seqs), BF16),
             pltpu.VMEM((neb, cols * ein, seqs), BF16),
             pltpu.VMEM((neb * CO, ein * cz), BF16),
             pltpu.VMEM((rb, neb, CO, cols * ein), BF16),
-            dma((nd,)),
-            dma((nd,)),
+            dma((nd, rd)),
+            dma((nd, rd)),
             dma((nh, 3)),
             dma((nh, 3)),
             dma((n,)),
             dma((n,)),
-            dma((nd,)),
-            dma((nd,)),
-            dma((nh,)),
-            dma((nh,)),
+            dma((nd, rd)),
+            dma((nd, rd)),
+            dma((nh, rd)),
+            dma((nh, rd)),
         ],
         compiler_params=pltpu.CompilerParams(
             collective_id=0, has_side_effects=True, vmem_limit_bytes=56 * 1024 * 1024

time: 43.6 us -> 38.2 us (0.88)
  Pallas kernels: 40.4 us -> 35 us
    pallas_call x1, Pallas kernels: 40.4 us -> 35 us  [per_device(): pl.pallas_call(functools.partial(kernel, nd, nh), out_shape=(jax.ShapeDty...]
where the time goes in v2:
time: 38.2 us; the launch traced here: 38.1 us
  Pallas kernels  35 us (92%)
  local copies, waits for them, and re-layouts  2.42 us (6%)
  between operations  0.65 us (2%)
    pallas_call x1, Pallas kernels, per_device(): pl.pallas_call(functools.partial(kernel, nd, nh), out_shape=(jax.ShapeDty...  35 us
    unnamed x4, local copies, waits for them, and re-layouts  2.42 us

profile of v2, /device:TPU:0, one launch (start us, length us, event | category | flops | bytes accessed | tf_op | source)
XLA Modules:
  0.0 38.1 jit_solution(11245374032622489324)
XLA Ops:
  0.6 35.0 %shard_map.149 = (bf16[4,128,256]{2,1,0:T(8,128)(2,1)}, f32[16,32,128]{2,1,0:T(8,128)}) custom-call(bf16[16,128,256]{2,1,0:T(8,128)(2,1)} %msa.1, s32[1,128]{1,0:T(1,128)} %bitcast.20, s32[1,128]{1,0:T(1,128)} %bitcast.21, f32[1,256]{1,0:T(1,128)} %bitcast.15, f32[1,256]{1,0:T(1,128)} %bitcast.16, bf16[4,64,256]{2,1,0:T(8,128)(2,1)} %bitcast.13, ...), custom_call_target="tpu_custom_call" | custom-call | tf_op jit(solution)/shard_map/pallas_call | solution.py:383
  35.7 0.0 copy-start
  35.7 1.7 %copy.18 = bf16[4,128,256]{2,1,0:T(8,128)(2,1)} copy(bf16[4,128,256]{2,1,0:T(8,128)(2,1)} %get-tuple-element.4) | data formatting | bytes 524288
  37.4 0.0 copy-done
  37.4 0.7 %copy.19 = f32[16,32,128]{2,1,0:T(8,128)} copy(f32[16,32,128]{2,1,0:T(8,128)S(1)} %copy-done) | data formatting | bytes 524288
Async XLA Ops:
  35.7 1.7 %copy-start = (f32[16,32,128]{2,1,0:T(8,128)S(1)}, f32[16,32,128]{2,1,0:T(8,128)}, u32[]{:S(2)}) copy-start(f32[16,32,128]{2,1,0:T(8,128)} %get-tuple-element.5) | copy-start | bytes 786436

commit v3 on v2

--- a/solution.py
+++ b/solution.py
@@ -38,49 +38,56 @@
 def kernel(
     nd,
     nh,
-    msa,
-    homolog,
-    amino,
-    gain1,
-    bias1,
-    w_local,
-    gate_local,
-    wf_local,
-    final_bias,
-    gain2,
-    bias2,
-    factors,
-    w_pair,
-    pair_bias,
-    align_out,
-    pair_out,
-    send1,
-    recv1,
-    w_all,
-    wf_all,
-    gate_rows,
-    gate_all,
-    aligned,
-    cbuf,
-    crecv,
-    lbuf,
-    rstack,
-    right_in,
-    left_all,
-    right_all,
-    w_r,
-    obuf,
-    s1,
-    r1,
-    s2,
-    r2,
-    s3,
-    r3,
-    s4,
-    r4,
-    s5,
-    r5,
+    *refs,
 ):
+    args = refs[:14]
+    align_out, pair_out = refs[14:16]
+    held = refs[16:30]
+    (
+        msa,
+        homolog,
+        amino,
+        gain1,
+        bias1,
+        w_local,
+        gate_local,
+        wf_local,
+        final_bias,
+        gain2,
+        bias2,
+        factors,
+        w_pair,
+        pair_bias,
+    ) = held
+    (
+        load_sem,
+        send1,
+        recv1,
+        w_all,
+        wf_all,
+        gate_rows,
+        gate_all,
+        aligned,
+        cbuf,
+        crecv,
+        lbuf,
+        rstack,
+        right_in,
+        left_all,
+        right_all,
+        w_r,
+        obuf,
+        s1,
+        r1,
+        s2,
+        r2,
+        s3,
+        r3,
+        s4,
+        r4,
+        s5,
+        r5,
+    ) = refs[30:]
     md = lax.axis_index("dap")
     mh = lax.axis_index("head")
     sl, res, ch = msa.shape
@@ -111,70 +118,19 @@
         to = (lax.rem(md + k, nd), mh)
         pl.semaphore_signal(barrier, inc=1, device_id=to, device_id_type=MESH)
 
+    loads = [pltpu.make_async_copy(args[i], held[i], load_sem.at[i]) for i in range(14)]
+    for c in loads:
+        c.start()
+    loads[0].wait()
+
     ri = iota((rows, sl * rb), 0)
     ci = iota((rows, sl * rb), 1)
     pick = one_hot(ci == lax.rem(ri, sl) * rb + mh * rd + ri // sl)
     for d in range(nd):
         block = msa[:, d * rb : (d + 1) * rb, :].reshape(sl * rb, ch)
         send1[d] = dot(pick, block, 1, 0).astype(BF16)
-    pl.semaphore_wait(barrier, nd + nh - 2)
-
-    copies = []
-
-    def start(src, dst, ss, rs, to):
-        c = pltpu.make_async_remote_copy(
-            src_ref=src, dst_ref=dst, send_sem=ss, recv_sem=rs, device_id=to, device_id_type=MESH
-        )
-        c.start()
-        copies.append(c)
-        return c
-
-    def head_rows(g):
-        return pl.ds(pl.multiple_of(g * hl, hl), hl)
-
-    def send_weights(g, own, idx, to):
-        at = head_rows(g)
-        src = (
-            (w_local, wf_local, gate_local)
-            if own
-            else (w_all.at[:, at, :], wf_all.at[at, :], gate_rows.at[g])
-        )
-        dst = (w_all.at[:, at, :], wf_all.at[at, :], gate_rows.at[g])
-        for j in range(3):
-            start(src[j], dst[j], s2.at[idx, j], r2.at[g, j], (md, to))
-
-    def wait_weights(g):
-        at = head_rows(g)
-        src = (w_local, wf_local, gate_local)
-        dst = (w_all.at[:, at, :], wf_all.at[at, :], gate_rows.at[g])
-        for j in range(3):
-            pltpu.make_async_remote_copy(
-                src_ref=src[j],
-                dst_ref=dst[j],
-                send_sem=s2.at[0, j],
-                recv_sem=r2.at[g, j],
-                device_id=(md, partner),
-                device_id_type=MESH,
-            ).wait_recv()
-
-    mine = head_rows(mh)
-    pairs = nh // 2
-    for k in range(1, pairs):
-        send_weights(mh, True, k, lax.rem(mh + 2 * k, nh))
-    send_weights(mh, True, 0, partner)
-    msas = []
-    for r in range(rd):
-        at = slice(r * sl, (r + 1) * sl)
-        for k in range(1, nd):
-            to = lax.rem(md + k, nd)
-            msas.append(
-                start(send1.at[to, at], recv1.at[md, at], s1.at[k, r], r1.at[k, r], (to, mh))
-            )
-
-    recv1[md] = send1[md]
-    w_all[:, mine, :] = w_local[...]
-    wf_all[mine, :] = wf_local[...]
-    gate_rows[mh] = gate_local[...]
+    for c in loads[1:]:
+        c.wait()
     for eb in range(neb):
         for e in range(ein):
             w_r[eb * CO : (eb + 1) * CO, e * cz : (e + 1) * cz] = w_pair[
@@ -190,6 +146,64 @@
     penalty = jnp.broadcast_to(jnp.where(seq_col > 0.5, 0.0, -1e9), (seqs, seqs))
     own = one_hot(iota((8, res), 1) == md * rb + mh * rd + iota((8, res), 0))
     own_keep = dot(own, res_wide, 1, 1)[:, :1]
+    pl.semaphore_wait(barrier, nd + nh - 2)
+
+    copies = []
+
+    def start(src, dst, ss, rs, to):
+        c = pltpu.make_async_remote_copy(
+            src_ref=src, dst_ref=dst, send_sem=ss, recv_sem=rs, device_id=to, device_id_type=MESH
+        )
+        c.start()
+        copies.append(c)
+        return c
+
+    def head_rows(g):
+        return pl.ds(pl.multiple_of(g * hl, hl), hl)
+
+    def send_weights(g, own, idx, to):
+        at = head_rows(g)
+        src = (
+            (w_local, wf_local, gate_local)
+            if own
+            else (w_all.at[:, at, :], wf_all.at[at, :], gate_rows.at[g])
+        )
+        dst = (w_all.at[:, at, :], wf_all.at[at, :], gate_rows.at[g])
+        for j in range(3):
+            start(src[j], dst[j], s2.at[idx, j], r2.at[g, j], (md, to))
+
+    def wait_weights(g):
+        at = head_rows(g)
+        src = (w_local, wf_local, gate_local)
+        dst = (w_all.at[:, at, :], wf_all.at[at, :], gate_rows.at[g])
+        for j in range(3):
+            pltpu.make_async_remote_copy(
+                src_ref=src[j],
+                dst_ref=dst[j],
+                send_sem=s2.at[0, j],
+                recv_sem=r2.at[g, j],
+                device_id=(md, partner),
+                device_id_type=MESH,
+            ).wait_recv()
+
+    mine = head_rows(mh)
+    pairs = nh // 2
+    for k in range(1, pairs):
+        send_weights(mh, True, k, lax.rem(mh + 2 * k, nh))
+    send_weights(mh, True, 0, partner)
+    msas = []
+    for r in range(rd):
+        at = slice(r * sl, (r + 1) * sl)
+        for k in range(1, nd):
+            to = lax.rem(md + k, nd)
+            msas.append(
+                start(send1.at[to, at], recv1.at[md, at], s1.at[k, r], r1.at[k, r], (to, mh))
+            )
+
+    recv1[md] = send1[md]
+    w_all[:, mine, :] = w_local[...]
+    wf_all[mine, :] = wf_local[...]
+    gate_rows[mh] = gate_local[...]
     for k in range(1, pairs):
         g = lax.rem(mh + nh - 2 * k, nh)
         wait_weights(g)
@@ -227,15 +241,13 @@
         key = dot(w_all[1], normed, 1, 1).astype(BF16)
         val = dot(w_all[2], normed, 1, 1).astype(BF16)
         gate = jax.nn.sigmoid(dot(w_all[3], normed, 1, 1) + gate_all[:, :1])
-        parts = []
-        for h in range(heads):
-            at = slice(h * DH, (h + 1) * DH)
-            scores = dot(key[at], q[at], 0, 0) + penalty
-            top = jnp.max(scores, 0, keepdims=True)
-            w = jnp.exp(scores - top)
-            total = jnp.sum(w, 0, keepdims=True)
-            probs = (w * (1.0 / total)).astype(BF16)
-            parts.append((dot(val[at], probs, 1, 0) * gate[at]).astype(BF16))
+        ats = [slice(h * DH, (h + 1) * DH) for h in range(heads)]
+        scores = [dot(key[at], q[at], 0, 0) + penalty for at in ats]
+        tops = [jnp.max(v, 0, keepdims=True) for v in scores]
+        ws = [jnp.exp(v - top) for v, top in zip(scores, tops)]
+        totals = [1.0 / jnp.sum(w, 0, keepdims=True) for w in ws]
+        probs = [(w * t).astype(BF16) for w, t in zip(ws, totals)]
+        parts = [(dot(val[at], p, 1, 0) * gate[at]).astype(BF16) for at, p in zip(ats, probs)]
         attended = jnp.concatenate(parts, 0)
         update = dot(attended, wf_all[...], 0, 0)
         out = (x + update + final_bias[...]).astype(BF16)
@@ -380,15 +392,33 @@
     factors = tensor_product_factors.transpose(1, 2, 0).reshape(2 * CO, ch)
     dma = pltpu.SemaphoreType.DMA
     vmem = pl.BlockSpec(memory_space=pltpu.VMEM)
+    operands = (
+        multiple_aligned_family,
+        row(homolog_present_flags),
+        row(amino_present_flags),
+        row(focus_layernorm_scaling),
+        row(focus_layernorm_offset),
+        w_local,
+        row(sigmoid_switch_offset),
+        focus_final_matrix,
+        row(focus_final_offset),
+        row(tensor_layernorm_scaling),
+        row(tensor_layernorm_offset),
+        factors,
+        tensor_final_matrix,
+        row(tensor_final_offset),
+    )
     return pl.pallas_call(
         functools.partial(kernel, nd, nh),
         out_shape=(
-            jax.ShapeDtypeStruct((sg, res, ch), BF16),
-            jax.ShapeDtypeStruct((rb, cols, cz), F32),
+            pltpu.VMEM((sg, res, ch), BF16),
+            pltpu.VMEM((rb, cols, cz), F32),
         ),
-        in_specs=[vmem] * 14,
+        in_specs=[pl.BlockSpec(memory_space=pl.ANY)] * 14,
         out_specs=(vmem, vmem),
-        scratch_shapes=[
+        scratch_shapes=[pltpu.VMEM(v.shape, v.dtype) for v in operands]
+        + [
+            dma((14,)),
             pltpu.VMEM((nd, rd * sl, ch), BF16),
             pltpu.VMEM((nd, rd * sl, ch), BF16),
             pltpu.VMEM((4, nh * hl, ch), BF16),
@@ -419,22 +449,7 @@
         compiler_params=pltpu.CompilerParams(
             collective_id=0, has_side_effects=True, vmem_limit_bytes=56 * 1024 * 1024
         ),
-    )(
-        multiple_aligned_family,
-        row(homolog_present_flags),
-        row(amino_present_flags),
-        row(focus_layernorm_scaling),
-        row(focus_layernorm_offset),
-        w_local,
-        row(sigmoid_switch_offset),
-        focus_final_matrix,
-        row(focus_final_offset),
-        row(tensor_layernorm_scaling),
-        row(tensor_layernorm_offset),
-        factors,
-        tensor_final_matrix,
-        row(tensor_final_offset),
-    )
+    )(*operands)
 
 
 def solution(mesh):

time: 38.2 us -> 30.4 us (0.80)
  Pallas kernels: 35 us -> 28.2 us
  local copies, waits for them, and re-layouts: 2.42 us -> 1.41 us
    pallas_call x1, Pallas kernels: 35 us -> 28.2 us  [per_device(): pl.pallas_call(functools.partial(kernel, nd, nh), out_shape=(pltpu.VMEM((...]
    unnamed x4 -> x2, local copies, waits for them, and re-layouts: 2.42 us -> 1.41 us
where the time goes in v3:
time: 30.4 us; the launch traced here: 30.3 us
  Pallas kernels  28.2 us (93%)
  local copies, waits for them, and re-layouts  1.41 us (5%)
  between operations  0.64 us (2%)
    pallas_call x1, Pallas kernels, per_device(): pl.pallas_call(functools.partial(kernel, nd, nh), out_shape=(pltpu.VMEM((...  28.2 us
    unnamed x2, local copies, waits for them, and re-layouts  1.41 us

profile of v3, /device:TPU:0, one launch (start us, length us, event | category | flops | bytes accessed | tf_op | source)
XLA Modules:
  0.0 30.3 jit_solution(12928450579448277985)
XLA Ops:
  0.6 28.2 %shard_map.149 = (bf16[4,128,256]{2,1,0:T(8,128)(2,1)S(1)}, f32[16,32,128]{2,1,0:T(8,128)S(1)}) custom-call(bf16[16,128,256]{2,1,0:T(8,128)(2,1)} %refs_0_.1, s32[1,128]{1,0:T(1,128)} %bitcast.20, s32[1,128]{1,0:T(1,128)} %bitcast.21, f32[1,256]{1,0:T(1,128)} %bitcast.15, f32[1,256]{1,0:T(1,128)} %bitcast.16, bf16[4,64,256]{2,1,0:T(8,128)(2,1)} %bitcast.13, ...), custom_call_target="tpu_custom_call" | custom-call | tf_op jit(solution)/shard_map/pallas_call | solution.py:411
  28.9 0.7 %copy.18 = bf16[4,128,256]{2,1,0:T(8,128)(2,1)} copy(bf16[4,128,256]{2,1,0:T(8,128)(2,1)S(1)} %get-tuple-element.2) | data formatting | bytes 524288
  29.6 0.7 %copy.19 = f32[16,32,128]{2,1,0:T(8,128)} copy(f32[16,32,128]{2,1,0:T(8,128)S(1)} %get-tuple-element.3) | data formatting | bytes 524288
